TPU v7x, 128 devices: a whole 4x4x4 slice. The times are simulated.
128 devices in a mesh: tm: 8 (over z_hi, x), space: 16 (over z_lo, y, core).
Axes of the slice: x: 4, y: 4, z: 4 (z_hi: 2, z_lo: 2; z = z_hi * 2 + z_lo), core: 2. Of those that a mesh axis runs over, the one named last changes fastest.
Arguments:
- snapshots: float32 [256, 3, 16, 32, 128], P('tm', None, 'space'), may hold values from -6 to 6
- coeffs: float32 [256, 128], replicated, may hold values from -0.375 to 0.375
- pair_table: int32 [4096, 2], replicated, may hold values from 0 to 127
Outputs:
- tensor: float32 [4096, 128], P(('tm', 'space'))
Inputs may be any that keep to these rules, and one draw needn't show every extreme that they name: `pair_table`: column 0 names the carrying mode, column 1 the carried mode.
All inputs are finite; a program needn't handle non-finite values.
Results may differ from a plain program's by a relative error of at most 0.00016.
Values sent between devices are 32-bit elements; how exact they have to be, the bound alone decides.
A program may use at most 192 MiB of HBM per device.

v0:
```python
import math
import jax
import jax.numpy as jnp
from jax import lax
from jax.sharding import PartitionSpec as P


def padded(block, sides, width):
    for axis, dim in sides:
        count = lax.axis_size(axis)
        forward = [(i, i + 1) for i in range(count - 1)]
        forward.append((count - 1, 0))
        backward = [(target, source) for source, target in forward]
        low = lax.ppermute(
            lax.slice_in_dim(block, block.shape[dim] - width, None, axis=dim), axis, forward
        )
        high = lax.ppermute(lax.slice_in_dim(block, 0, width, axis=dim), axis, backward)
        block = jnp.concatenate([low, block, high], axis=dim)
    return block


def slope_field(center, padded_x, padded_y):
    stream_slope = (padded_x[:, :, 2:] - padded_x[:, :, :-2]) * 0.5
    normal_slope = (padded_y[:, :, :, 2:] - padded_y[:, :, :, :-2]) * 0.5
    span_slope = (jnp.roll(center, -1, 4) - jnp.roll(center, 1, 4)) * 0.5
    return jnp.stack([stream_slope, normal_slope, span_slope], axis=1)


def pair_block(pair_rows, table_modes, table_slopes, flat_modes):
    modes_count = table_modes.shape[0]
    cells = flat_modes.shape[2]
    group_size = pair_rows.shape[0]
    levels = lax.broadcasted_iota(jnp.int32, (group_size, modes_count), 1)
    first_pick = (pair_rows[:, 0:1] == levels).astype(jnp.float32)
    second_pick = (pair_rows[:, 1:2] == levels).astype(jnp.float32)
    first_modes = jnp.dot(
        first_pick, table_modes, precision=lax.Precision.HIGHEST, preferred_element_type=jnp.float32
    ).reshape(group_size, 3, cells)
    second_slopes = jnp.dot(
        second_pick,
        table_slopes,
        precision=lax.Precision.HIGHEST,
        preferred_element_type=jnp.float32,
    ).reshape(group_size, 3, 3, cells)
    convection = jnp.einsum(
        "bdl,bdcl->bcl", first_modes, second_slopes, precision=lax.Precision.HIGHEST
    )
    return jnp.einsum("bcl,kcl->bk", convection, flat_modes, precision=lax.Precision.HIGHEST)


def pair_terms(pair_source, flat_modes, flat_slopes, factor, row_count):
    modes_count = flat_modes.shape[0]
    table_modes = flat_modes.reshape(modes_count, -1)
    table_slopes = flat_slopes.reshape(modes_count, -1)
    group_size = math.gcd(row_count, 64)
    grouped = pair_source.reshape(row_count // group_size, group_size, 2)

    def one_group(group_rows):
        return pair_block(group_rows, table_modes, table_slopes, flat_modes)

    result = lax.map(one_group, grouped)
    return result.reshape(row_count, -1) * factor


def shards(snapshots, coeffs, pair_table):
    mode_field = jnp.einsum(
        "sk,scxyz->kcxyz",
        coeffs,
        lax.all_to_all(snapshots, "tm", split_axis=3, concat_axis=0, tiled=True),
        precision=lax.Precision.HIGHEST,
    )
    tm_count = lax.axis_size("tm")
    space_count = lax.axis_size("space")
    total_cells = (
        mode_field.shape[2] * mode_field.shape[3] * mode_field.shape[4] * tm_count * space_count
    )
    factor = float(total_cells) ** (-0.5)
    modes_count = mode_field.shape[0]
    whole_slab = lax.all_gather(mode_field, "tm", axis=3, tiled=True)
    padded_x = padded(whole_slab, (("space", 2),), 1)
    padded_y = jnp.pad(whole_slab, ((0, 0), (0, 0), (0, 0), (1, 1), (0, 0)))
    slopes = slope_field(whole_slab, padded_x, padded_y)
    flat_modes = whole_slab.reshape(modes_count, 3, -1)
    flat_slopes = slopes.reshape(modes_count, 3, 3, -1)
    owned_count = pair_table.shape[0] // tm_count
    owned = lax.dynamic_slice_in_dim(pair_table, lax.axis_index("tm") * owned_count, owned_count, 0)
    tensor = lax.psum_scatter(
        pair_terms(
            owned,
            flat_modes,
            flat_slopes,
            factor,
            lax.axis_size("space") * (owned_count // space_count),
        ),
        "space",
        scatter_dimension=0,
        tiled=True,
    )
    return tensor


def solution(mesh):
    placed = (P("tm", None, "space", None, None), P(), P())
    return jax.shard_map(
        shards, mesh=mesh, in_specs=placed, out_specs=P(("tm", "space"), None), check_vma=False
    )
```

profile of v0, /device:TPU:0, one launch (start us, length us, event | category | flops | bytes accessed | tf_op | source)
XLA Modules:
  0.0 765.1 jit_solution(8880501986956262538)
XLA Ops:
  8.9 30.3 %all_to_all.15 = f32[32,3,1,32,128]{4,0,2,1,3:T(8,128)S(1)} all-to-all(f32[32,3,1,32,128]{4,0,2,1,3:T(8,128)S(1)} %copy.44), channel_id=1, replica_groups=mesh['tm'=8,'space'=16] {'tm'}, dimensions={3} | all-to-all | bytes 3145728 | tf_op jit(solution)/shard_map/all_to_all | solution.py:69
  41.5 86.9 %all-gather.3.cloned.1.call-done = f32[128,3,32,128]{3,0,2,1:T(8,128)} async-done(((f32[128,3,4,128]{3,0,2,1:T(8,128)}), f32[128,3,32,128]{3,0,2,1:T(8,128)}) %all-gather.3.cloned.1.call-update) | async-done | bytes 6291472 | tf_op jit(solution)/shard_map/all_gather | solution.py:79
  130.8 6.7 copy.51
  137.5 6.6 copy.55
  144.1 6.8 copy.56
  150.8 9.3 %fusion.15 = f32[128,1,3,1,32,128]{5,0,4,2,3,1:T(8,128)} fusion(f32[128,3,1,32,128]{4,0,3,1,2:T(8,128)} %bitcast.73), kind=kLoop, calls=%fused_computation.20 | loop fusion | flops 3145728 | bytes 12582912 | tf_op jit(solution)/shard_map/stack | solution.py:26
  160.2 6.6 slice_bitcast_fusion.3
  166.8 6.7 slice_bitcast_fusion.2
  173.5 10.1 %fusion.16 = f32[128,1,3,1,32,128]{5,0,4,2,3,1:T(8,128)S(1)} fusion(f32[128,1,3,1,32,1]{5,0,4,2,3,1:T(8,128)} %get-tuple-element.77, f32[128,1,3,1,32,127]{5,0,4,2,3,1:T(8,128)} %get-tuple-element.79, f32[128,1,3,1,32,127]{5,0,4,2,3,1:T(8,128)} %get-tuple-element.78, f32[128,1,3,1,32,1]{5,0,4,2,3,1:T(8,128)} %get-tuple-element.76), kind=kLoop, calls=%fused_computation.26 | loop fusion | flops 6291456 | bytes 18874368 | tf_op jit(solution)/shard_map/mul | solution.py:25
  183.6 15.2 %collective-permute-done = f32[128,3,1,32,128]{4,0,3,1,2:T(8,128)} collective-permute-done((f32[128,3,1,32,128]{4,0,3,1,2:T(8,128)}, f32[128,3,1,32,128]{4,0,3,1,2:T(8,128)}, u32[]{:S(2)}, u32[]{:S(2)}) %collective-permute-start) | collective-permute-done | bytes 6291488 | tf_op jit(solution)/shard_map/ppermute | solution.py:17
  202.8 6.0 multiply_bitcast_fusion
  208.8 6.7 pad_maximum_fusion
  215.5 18.7 %copy.50 = f32[128,3,3,1,32,128]{0,5,4,2,1,3:T(8,128)} copy(f32[128,3,3,1,32,128]{5,0,4,2,3,1:T(8,128)} %pad_maximum_fusion) | data formatting | bytes 37748736 | tf_op jit(solution)/shard_map/stack | solution.py:26
  234.2 18.7 %copy.54 = f32[128,36864]{1,0:T(8,128)} copy(f32[128,36864]{0,1:T(8,128)} %bitcast.78) | data formatting | bytes 37748736 | tf_op jit(solution)/shard_map/while | solution.py:61
  252.9 447.4 %while.10 = (s32[]{:T(128)}, f32[8,64,128]{2,1,0:T(8,128)S(1)}, s32[8,64,2]{1,0,2:T(8,128)S(1)}, f32[128,36864]{1,0:T(8,128)}, f32[128,12288]{1,0:T(8,128)}, /*index=5*/f32[128,3,4096]{2,0,1:T(8,128)}, s32[]{:T(128)}) while((s32[]{:T(128)}, f32[8,64,128]{2,1,0:T(8,128)S(1)}, s32[8,64,2]{1,0,2:T(8,128)S(1)}, f32[128,36864]{1,0:T(8,128)}, ...), condition=%wide.region_1.2_spmd, body=%wide.region_0.1_spmd.sunk | while | flops 6043746304 | bytes 89164368 | solution.py:61
  252.9 13.5 %fusion.34 = f32[64,36864]{1,0:T(8,128)} fusion(f32[128,36864]{1,0:T(8,128)} %get-tuple-element.138, s32[64]{0:T(128)S(1)} %get-tuple-element.119), kind=kOutput, calls=%fused_computation.8.clone.1 | convolution fusion | flops 3623886848 | bytes 28311808 | tf_op jit(solution)/shard_map/while/body/eval_jaxpr/dot_general | solution.py:39
  266.5 12.7 %reshape.108 = f32[64,3,3,4096]{3,2,1,0:T(4,128)} reshape(f32[64,36864]{1,0:T(8,128)} %fusion.34) | data formatting | bytes 18874368 | tf_op jit(solution)/shard_map/while/body/eval_jaxpr/reshape | solution.py:44
  287.4 12.6 %multiply_reduce_fusion.2 = f32[64,4096,3]{1,2,0:T(4,128)S(1)} fusion(f32[64,3,3,4096]{3,2,1,0:T(4,128)} %reshape.108, f32[64,4096,3]{1,2,0:T(4,128)} %bitcast.70), kind=kLoop, calls=%fused_computation.clone.1 | loop fusion | flops 3932160 | bytes 15728640 | tf_op jit(solution)/shard_map/while
  299.9 8.9 %fusion.36 = f32[8,64,128]{2,1,0:T(8,128)S(1)} fusion(f32[8,64,128]{2,1,0:T(8,128)S(1)} %get-tuple-element.129, s32[]{:T(128)} %get-tuple-element.128, f32[128,3,4096]{2,0,1:T(8,128)} %get-tuple-element.140, f32[64,4096,3]{1,2,0:T(4,128)S(1)} %multiply_reduce_fusion.2), kind=kOutput, calls=%fused_computation.5.clone.1 | convolution fusion | flops 1207959552 | bytes 10518532 | tf_op jit(solution)/shard_map/while/body/eval_jaxpr/bcl,kcl->bk/dot_general | solution.py:48
  308.9 13.5 %fusion.34 = f32[64,36864]{1,0:T(8,128)} fusion(f32[128,36864]{1,0:T(8,128)} %get-tuple-element.138, s32[64]{0:T(128)S(1)} %get-tuple-element.119), kind=kOutput, calls=%fused_computation.8.clone.1 | convolution fusion | flops 3623886848 | bytes 28311808 | tf_op jit(solution)/shard_map/while/body/eval_jaxpr/dot_general | solution.py:39
  322.4 12.7 %reshape.108 = f32[64,3,3,4096]{3,2,1,0:T(4,128)} reshape(f32[64,36864]{1,0:T(8,128)} %fusion.34) | data formatting | bytes 18874368 | tf_op jit(solution)/shard_map/while/body/eval_jaxpr/reshape | solution.py:44
  343.3 12.6 %multiply_reduce_fusion.2 = f32[64,4096,3]{1,2,0:T(4,128)S(1)} fusion(f32[64,3,3,4096]{3,2,1,0:T(4,128)} %reshape.108, f32[64,4096,3]{1,2,0:T(4,128)} %bitcast.70), kind=kLoop, calls=%fused_computation.clone.1 | loop fusion | flops 3932160 | bytes 15728640 | tf_op jit(solution)/shard_map/while
  355.9 8.9 %fusion.36 = f32[8,64,128]{2,1,0:T(8,128)S(1)} fusion(f32[8,64,128]{2,1,0:T(8,128)S(1)} %get-tuple-element.129, s32[]{:T(128)} %get-tuple-element.128, f32[128,3,4096]{2,0,1:T(8,128)} %get-tuple-element.140, f32[64,4096,3]{1,2,0:T(4,128)S(1)} %multiply_reduce_fusion.2), kind=kOutput, calls=%fused_computation.5.clone.1 | convolution fusion | flops 1207959552 | bytes 10518532 | tf_op jit(solution)/shard_map/while/body/eval_jaxpr/bcl,kcl->bk/dot_general | solution.py:48
  364.8 13.5 %fusion.34 = f32[64,36864]{1,0:T(8,128)} fusion(f32[128,36864]{1,0:T(8,128)} %get-tuple-element.138, s32[64]{0:T(128)S(1)} %get-tuple-element.119), kind=kOutput, calls=%fused_computation.8.clone.1 | convolution fusion | flops 3623886848 | bytes 28311808 | tf_op jit(solution)/shard_map/while/body/eval_jaxpr/dot_general | solution.py:39
  378.3 12.7 %reshape.108 = f32[64,3,3,4096]{3,2,1,0:T(4,128)} reshape(f32[64,36864]{1,0:T(8,128)} %fusion.34) | data formatting | bytes 18874368 | tf_op jit(solution)/shard_map/while/body/eval_jaxpr/reshape | solution.py:44
  399.2 12.6 %multiply_reduce_fusion.2 = f32[64,4096,3]{1,2,0:T(4,128)S(1)} fusion(f32[64,3,3,4096]{3,2,1,0:T(4,128)} %reshape.108, f32[64,4096,3]{1,2,0:T(4,128)} %bitcast.70), kind=kLoop, calls=%fused_computation.clone.1 | loop fusion | flops 3932160 | bytes 15728640 | tf_op jit(solution)/shard_map/while
  411.8 8.9 %fusion.36 = f32[8,64,128]{2,1,0:T(8,128)S(1)} fusion(f32[8,64,128]{2,1,0:T(8,128)S(1)} %get-tuple-element.129, s32[]{:T(128)} %get-tuple-element.128, f32[128,3,4096]{2,0,1:T(8,128)} %get-tuple-element.140, f32[64,4096,3]{1,2,0:T(4,128)S(1)} %multiply_reduce_fusion.2), kind=kOutput, calls=%fused_computation.5.clone.1 | convolution fusion | flops 1207959552 | bytes 10518532 | tf_op jit(solution)/shard_map/while/body/eval_jaxpr/bcl,kcl->bk/dot_general | solution.py:48
  420.7 13.5 %fusion.34 = f32[64,36864]{1,0:T(8,128)} fusion(f32[128,36864]{1,0:T(8,128)} %get-tuple-element.138, s32[64]{0:T(128)S(1)} %get-tuple-element.119), kind=kOutput, calls=%fused_computation.8.clone.1 | convolution fusion | flops 3623886848 | bytes 28311808 | tf_op jit(solution)/shard_map/while/body/eval_jaxpr/dot_general | solution.py:39
  434.2 12.7 %reshape.108 = f32[64,3,3,4096]{3,2,1,0:T(4,128)} reshape(f32[64,36864]{1,0:T(8,128)} %fusion.34) | data formatting | bytes 18874368 | tf_op jit(solution)/shard_map/while/body/eval_jaxpr/reshape | solution.py:44
  455.1 12.6 %multiply_reduce_fusion.2 = f32[64,4096,3]{1,2,0:T(4,128)S(1)} fusion(f32[64,3,3,4096]{3,2,1,0:T(4,128)} %reshape.108, f32[64,4096,3]{1,2,0:T(4,128)} %bitcast.70), kind=kLoop, calls=%fused_computation.clone.1 | loop fusion | flops 3932160 | bytes 15728640 | tf_op jit(solution)/shard_map/while
  467.7 8.9 %fusion.36 = f32[8,64,128]{2,1,0:T(8,128)S(1)} fusion(f32[8,64,128]{2,1,0:T(8,128)S(1)} %get-tuple-element.129, s32[]{:T(128)} %get-tuple-element.128, f32[128,3,4096]{2,0,1:T(8,128)} %get-tuple-element.140, f32[64,4096,3]{1,2,0:T(4,128)S(1)} %multiply_reduce_fusion.2), kind=kOutput, calls=%fused_computation.5.clone.1 | convolution fusion | flops 1207959552 | bytes 10518532 | tf_op jit(solution)/shard_map/while/body/eval_jaxpr/bcl,kcl->bk/dot_general | solution.py:48
  476.6 13.5 %fusion.34 = f32[64,36864]{1,0:T(8,128)} fusion(f32[128,36864]{1,0:T(8,128)} %get-tuple-element.138, s32[64]{0:T(128)S(1)} %get-tuple-element.119), kind=kOutput, calls=%fused_computation.8.clone.1 | convolution fusion | flops 3623886848 | bytes 28311808 | tf_op jit(solution)/shard_map/while/body/eval_jaxpr/dot_general | solution.py:39
  490.2 12.7 %reshape.108 = f32[64,3,3,4096]{3,2,1,0:T(4,128)} reshape(f32[64,36864]{1,0:T(8,128)} %fusion.34) | data formatting | bytes 18874368 | tf_op jit(solution)/shard_map/while/body/eval_jaxpr/reshape | solution.py:44
  511.1 12.6 %multiply_reduce_fusion.2 = f32[64,4096,3]{1,2,0:T(4,128)S(1)} fusion(f32[64,3,3,4096]{3,2,1,0:T(4,128)} %reshape.108, f32[64,4096,3]{1,2,0:T(4,128)} %bitcast.70), kind=kLoop, calls=%fused_computation.clone.1 | loop fusion | flops 3932160 | bytes 15728640 | tf_op jit(solution)/shard_map/while
  523.6 8.9 %fusion.36 = f32[8,64,128]{2,1,0:T(8,128)S(1)} fusion(f32[8,64,128]{2,1,0:T(8,128)S(1)} %get-tuple-element.129, s32[]{:T(128)} %get-tuple-element.128, f32[128,3,4096]{2,0,1:T(8,128)} %get-tuple-element.140, f32[64,4096,3]{1,2,0:T(4,128)S(1)} %multiply_reduce_fusion.2), kind=kOutput, calls=%fused_computation.5.clone.1 | convolution fusion | flops 1207959552 | bytes 10518532 | tf_op jit(solution)/shard_map/while/body/eval_jaxpr/bcl,kcl->bk/dot_general | solution.py:48
  532.6 13.5 %fusion.34 = f32[64,36864]{1,0:T(8,128)} fusion(f32[128,36864]{1,0:T(8,128)} %get-tuple-element.138, s32[64]{0:T(128)S(1)} %get-tuple-element.119), kind=kOutput, calls=%fused_computation.8.clone.1 | convolution fusion | flops 3623886848 | bytes 28311808 | tf_op jit(solution)/shard_map/while/body/eval_jaxpr/dot_general | solution.py:39
  546.1 12.7 %reshape.108 = f32[64,3,3,4096]{3,2,1,0:T(4,128)} reshape(f32[64,36864]{1,0:T(8,128)} %fusion.34) | data formatting | bytes 18874368 | tf_op jit(solution)/shard_map/while/body/eval_jaxpr/reshape | solution.py:44
  567.0 12.6 %multiply_reduce_fusion.2 = f32[64,4096,3]{1,2,0:T(4,128)S(1)} fusion(f32[64,3,3,4096]{3,2,1,0:T(4,128)} %reshape.108, f32[64,4096,3]{1,2,0:T(4,128)} %bitcast.70), kind=kLoop, calls=%fused_computation.clone.1 | loop fusion | flops 3932160 | bytes 15728640 | tf_op jit(solution)/shard_map/while
  579.6 8.9 %fusion.36 = f32[8,64,128]{2,1,0:T(8,128)S(1)} fusion(f32[8,64,128]{2,1,0:T(8,128)S(1)} %get-tuple-element.129, s32[]{:T(128)} %get-tuple-element.128, f32[128,3,4096]{2,0,1:T(8,128)} %get-tuple-element.140, f32[64,4096,3]{1,2,0:T(4,128)S(1)} %multiply_reduce_fusion.2), kind=kOutput, calls=%fused_computation.5.clone.1 | convolution fusion | flops 1207959552 | bytes 10518532 | tf_op jit(solution)/shard_map/while/body/eval_jaxpr/bcl,kcl->bk/dot_general | solution.py:48
  588.5 13.5 %fusion.34 = f32[64,36864]{1,0:T(8,128)} fusion(f32[128,36864]{1,0:T(8,128)} %get-tuple-element.138, s32[64]{0:T(128)S(1)} %get-tuple-element.119), kind=kOutput, calls=%fused_computation.8.clone.1 | convolution fusion | flops 3623886848 | bytes 28311808 | tf_op jit(solution)/shard_map/while/body/eval_jaxpr/dot_general | solution.py:39
  602.0 12.7 %reshape.108 = f32[64,3,3,4096]{3,2,1,0:T(4,128)} reshape(f32[64,36864]{1,0:T(8,128)} %fusion.34) | data formatting | bytes 18874368 | tf_op jit(solution)/shard_map/while/body/eval_jaxpr/reshape | solution.py:44
  622.9 12.6 %multiply_reduce_fusion.2 = f32[64,4096,3]{1,2,0:T(4,128)S(1)} fusion(f32[64,3,3,4096]{3,2,1,0:T(4,128)} %reshape.108, f32[64,4096,3]{1,2,0:T(4,128)} %bitcast.70), kind=kLoop, calls=%fused_computation.clone.1 | loop fusion | flops 3932160 | bytes 15728640 | tf_op jit(solution)/shard_map/while
  635.5 8.9 %fusion.36 = f32[8,64,128]{2,1,0:T(8,128)S(1)} fusion(f32[8,64,128]{2,1,0:T(8,128)S(1)} %get-tuple-element.129, s32[]{:T(128)} %get-tuple-element.128, f32[128,3,4096]{2,0,1:T(8,128)} %get-tuple-element.140, f32[64,4096,3]{1,2,0:T(4,128)S(1)} %multiply_reduce_fusion.2), kind=kOutput, calls=%fused_computation.5.clone.1 | convolution fusion | flops 1207959552 | bytes 10518532 | tf_op jit(solution)/shard_map/while/body/eval_jaxpr/bcl,kcl->bk/dot_general | solution.py:48
  644.4 13.5 %fusion.34 = f32[64,36864]{1,0:T(8,128)} fusion(f32[128,36864]{1,0:T(8,128)} %get-tuple-element.138, s32[64]{0:T(128)S(1)} %get-tuple-element.119), kind=kOutput, calls=%fused_computation.8.clone.1 | convolution fusion | flops 3623886848 | bytes 28311808 | tf_op jit(solution)/shard_map/while/body/eval_jaxpr/dot_general | solution.py:39
  657.9 12.7 %reshape.108 = f32[64,3,3,4096]{3,2,1,0:T(4,128)} reshape(f32[64,36864]{1,0:T(8,128)} %fusion.34) | data formatting | bytes 18874368 | tf_op jit(solution)/shard_map/while/body/eval_jaxpr/reshape | solution.py:44
  678.8 12.6 %multiply_reduce_fusion.2 = f32[64,4096,3]{1,2,0:T(4,128)S(1)} fusion(f32[64,3,3,4096]{3,2,1,0:T(4,128)} %reshape.108, f32[64,4096,3]{1,2,0:T(4,128)} %bitcast.70), kind=kLoop, calls=%fused_computation.clone.1 | loop fusion | flops 3932160 | bytes 15728640 | tf_op jit(solution)/shard_map/while
  691.4 8.9 %fusion.36 = f32[8,64,128]{2,1,0:T(8,128)S(1)} fusion(f32[8,64,128]{2,1,0:T(8,128)S(1)} %get-tuple-element.129, s32[]{:T(128)} %get-tuple-element.128, f32[128,3,4096]{2,0,1:T(8,128)} %get-tuple-element.140, f32[64,4096,3]{1,2,0:T(4,128)S(1)} %multiply_reduce_fusion.2), kind=kOutput, calls=%fused_computation.5.clone.1 | convolution fusion | flops 1207959552 | bytes 10518532 | tf_op jit(solution)/shard_map/while/body/eval_jaxpr/bcl,kcl->bk/dot_general | solution.py:48
  701.0 57.3 %reduce-scatter.2.cloned.1.call-done = f32[32,128]{1,0:T(8,128)} async-done(((f32[512,128]{1,0:T(8,128)}), f32[32,128]{1,0:T(8,128)}) %reduce-scatter.2.cloned.1.call-update) | async-done | bytes 16400 | tf_op jit(solution)/shard_map/reduce_scatter | solution.py:87
  (61 shorter events, 77.7 us)
Async XLA Ops:
  6.5 33.0 %copy-start = (f32[256,128]{1,0:T(8,128)S(1)}, f32[256,128]{1,0:T(8,128)}, u32[]{:S(2)}) copy-start(f32[256,128]{1,0:T(8,128)} %param.6) | copy-start | bytes 393220
  6.5 121.9 %all-gather.3.cloned.1.call-start = ((), (), s32[]{:S(2)}) async-start(), calls=%async_computation.3 | async-start | bytes 7077888 | tf_op jit(solution)/shard_map/all_gather | solution.py:79
  41.5 716.8 %reduce-scatter.2.cloned.1.call-start = ((), (), s32[]{:S(2)}) async-start(), calls=%async_computation.2 | async-start | bytes 278528 | tf_op jit(solution)/shard_map/reduce_scatter | solution.py:87
  128.4 70.4 %collective-permute-start = (f32[128,3,1,32,128]{4,0,3,1,2:T(8,128)}, f32[128,3,1,32,128]{4,0,3,1,2:T(8,128)}, u32[]{:S(2)}, u32[]{:S(2)}) collective-permute-start(f32[128,3,1,32,128]{4,0,3,1,2:T(8,128)} %bitcast.71), channel_id=1, source_target_pairs={{1,0},{2,1},{3,2},{4,3},{5,4},{6,5},{7,6},{8,7},{9,8},{10,9},{11,1... | collective-permute-start | bytes 18874376 | tf_op jit(solution)/shard_map/ppermute | solution.py:17
  130.0 72.8 %collective-permute-start.1 = (f32[128,3,1,32,128]{4,0,3,1,2:T(8,128)}, f32[128,3,1,32,128]{4,0,3,1,2:T(8,128)}, u32[]{:S(2)}, u32[]{:S(2)}) collective-permute-start(f32[128,3,1,32,128]{4,0,3,1,2:T(8,128)} %bitcast.72), channel_id=1, source_target_pairs={{0,1},{1,2},{2,3},{3,4},{4,5},{5,6},{6,7},{7,8},{8,9},{9,10},{10,1... | collective-permute-start | bytes 18874376 | tf_op jit(solution)/shard_map/ppermute | solution.py:14
  144.1 16.1 %slice-start = ((s8[6291456]{0:T(1024)(128)(4,1)}), s8[2097152]{0:T(1024)(128)(4,1)S(1)}, s32[]{:S(2)}) async-start(s8[6291456]{0:T(1024)(128)(4,1)} %bitcast.74), calls=%async_computation.4 | async-start | bytes 4194304
  150.8 9.3 %slice-start.1 = ((s8[6291456]{0:T(1024)(128)(4,1)}), s8[4194304]{0:T(1024)(128)(4,1)S(1)}, s32[]{:S(2)}) async-start(s8[6291456]{0:T(1024)(128)(4,1)} %bitcast.74), calls=%async_computation.5 | async-start | bytes 8388608
  173.5 35.3 %slice-start.2 = ((s8[6291456]{0:T(1024)(128)(4,1)}), s8[4194304]{0:T(1024)(128)(4,1)S(1)}, s32[]{:S(2)}) async-start(s8[6291456]{0:T(1024)(128)(4,1)} %bitcast.81), calls=%async_computation.6 | async-start | bytes 8388608
  173.5 35.3 %slice-start.3 = ((s8[6291456]{0:T(1024)(128)(4,1)}), s8[2097152]{0:T(1024)(128)(4,1)S(1)}, s32[]{:S(2)}) async-start(s8[6291456]{0:T(1024)(128)(4,1)} %bitcast.81), calls=%async_computation.7 | async-start | bytes 4194304
  700.3 58.0 %copy-start.1 = (f32[256,128]{1,0:T(8,128)S(1)}, f32[256,128]{1,0:T(8,128)}, u32[]{:S(2)}) copy-start(f32[256,128]{1,0:T(8,128)} %param.6) | copy-start | bytes 393220
Sparse Core Ops, SparseCore 0:
  41.6 86.7 all-gather.2
  701.2 57.0 reduce-scatter.1
where the time goes:
time: 769 us; the launch traced here: 765 us
  matrix products  217 us (28%)
  local copies, waits for them, and re-layouts  205 us (27%)
  waiting for transfers between devices  163 us (21%)
  other arithmetic  133 us (17%)
  blocking collectives  30.3 us (4%)
  between operations  13.5 us (2%)
    dot_general x8, matrix products, pair_block(): jnp.dot(second_pick, table_slopes, precision=lax.Precision.HIGHEST, prefe...  108 us
    reshape x8, local copies, waits for them, and re-layouts, pair_block(): second_slopes = jnp.dot(second_pick, table_slopes, precision=lax.Precisio...  101 us
    while x8, other arithmetic  101 us
    all_gather x1, waiting for transfers between devices, shards(): whole_slab = lax.all_gather(mode_field, 'tm', axis=3, tiled=True)  86.9 us
    dot_general x8, matrix products, pair_block(): jnp.einsum('bcl,kcl->bk', convection, flat_modes, precision=lax.Precision...  70.9 us
    reduce_scatter x1, waiting for transfers between devices, shards(): lax.psum_scatter(pair_terms(owned, flat_modes, flat_slopes, factor, lax.a...  57.3 us
    dot_general x8, matrix products, pair_block(): jnp.dot(first_pick, table_modes, precision=lax.Precision.HIGHEST, preferr...  36.1 us
    while x3, local copies, waits for them, and re-layouts, pair_terms(): result = lax.map(one_group, grouped)  32.1 us
  transfers between devices with their start and end apart: 4, of which 4 were waited for; matrix products, arithmetic and copies ran while one was open for 7% of the time, Pallas kernels for 0%

commit v1 on v0

--- a/solution.py
+++ b/solution.py
@@ -76,7 +76,9 @@
     )
     factor = float(total_cells) ** (-0.5)
     modes_count = mode_field.shape[0]
-    whole_slab = lax.all_gather(mode_field, "tm", axis=3, tiled=True)
+    whole_slab = jnp.concatenate(
+        lax.all_to_all(jnp.stack([mode_field] * lax.axis_size("tm")), "tm", 0, 0), axis=3
+    )
     padded_x = padded(whole_slab, (("space", 2),), 1)
     padded_y = jnp.pad(whole_slab, ((0, 0), (0, 0), (0, 0), (1, 1), (0, 0)))
     slopes = slope_field(whole_slab, padded_x, padded_y)

time: 769 us -> 762 us (level)
  blocking collectives: 30.3 us -> 105 us
  waiting for transfers between devices: 163 us -> 99.5 us
  other arithmetic: 133 us -> 117 us
    all_gather x1 -> x0, waiting for transfers between devices: 86.9 us -> none  [shards(): whole_slab = lax.all_gather(mode_field, 'tm', axis=3, tiled=True)]
    all_to_all x0 -> x1, blocking collectives: none -> 75.1 us  [shards(): lax.all_to_all(jnp.stack([mode_field] * lax.axis_size('tm')), 'tm', 0, 0)]
    ppermute x1, waiting for transfers between devices: 15.2 us -> 39.5 us  [padded(): lax.ppermute(lax.slice_in_dim(block, 0, width, axis=dim), axis, backward)]
    mul x1, other arithmetic: 10.1 us -> 1.64 us  [slope_field(): span_slope = (jnp.roll(center, -1, 4) - jnp.roll(center, 1, 4)) * 0.5]
    another operation x3, other arithmetic: 22 us -> 14.2 us  [slope_field(): return jnp.stack([stream_slope, normal_slope, span_slope], axis=1)]
  transfers between devices with their start and end apart: 4 -> 3, of which waited for: 4 -> 3; matrix products, arithmetic and copies ran while one was open for 7% -> 4% of each run, Pallas kernels for 0% -> 0%
where the time goes in v1:
time: 762 us; the launch traced here: 758 us
  matrix products  216 us (28%)
  local copies, waits for them, and re-layouts  205 us (27%)
  other arithmetic  117 us (15%)
  blocking collectives  105 us (14%)
  waiting for transfers between devices  99.5 us (13%)
  between operations  13.5 us (2%)
    dot_general x8, matrix products, pair_block(): jnp.dot(second_pick, table_slopes, precision=lax.Precision.HIGHEST, prefe...  108 us
    while x8, other arithmetic  101 us
    reshape x8, local copies, waits for them, and re-layouts, pair_block(): second_slopes = jnp.dot(second_pick, table_slopes, precision=lax.Precisio...  100 us
    all_to_all x1, blocking collectives, shards(): lax.all_to_all(jnp.stack([mode_field] * lax.axis_size('tm')), 'tm', 0, 0)  75.1 us
    dot_general x8, matrix products, pair_block(): jnp.einsum('bcl,kcl->bk', convection, flat_modes, precision=lax.Precision...  70.9 us
    reduce_scatter x1, waiting for transfers between devices, shards(): lax.psum_scatter(pair_terms(owned, flat_modes, flat_slopes, factor, lax.a...  55.9 us
    ppermute x1, waiting for transfers between devices, padded(): lax.ppermute(lax.slice_in_dim(block, 0, width, axis=dim), axis, backward)  39.5 us
    dot_general x8, matrix products, pair_block(): jnp.dot(first_pick, table_modes, precision=lax.Precision.HIGHEST, preferr...  36.1 us
  transfers between devices with their start and end apart: 3, of which 3 were waited for; matrix products, arithmetic and copies ran while one was open for 4% of the time, Pallas kernels for 0%

profile of v1, /device:TPU:0, one launch (start us, length us, event | category | flops | bytes accessed | tf_op | source)
XLA Modules:
  0.0 758.3 jit_solution(5783641225199809103)
XLA Ops:
  8.9 30.3 %all_to_all.20 = f32[32,3,1,32,128]{4,0,2,1,3:T(8,128)S(1)} all-to-all(f32[32,3,1,32,128]{4,0,2,1,3:T(8,128)S(1)} %copy.74), channel_id=1, replica_groups=mesh['tm'=8,'space'=16] {'tm'}, dimensions={3} | all-to-all | bytes 3145728 | tf_op jit(solution)/shard_map/all_to_all | solution.py:69
  42.2 75.1 %all_to_all.21 = f32[8,128,3,1,4,128]{1,4,5,2,3,0:T(4,128)S(1)} all-to-all(f32[8,128,3,1,4,128]{1,4,5,2,3,0:T(4,128)S(1)} %stack.8), channel_id=1, replica_groups=mesh['tm'=8,'space'=16] {'tm'}, dimensions={0} | all-to-all | bytes 12582912 | tf_op jit(solution)/shard_map/all_to_all | solution.py:80
  118.3 6.7 copy.80
  127.3 6.5 copy.90
  133.8 6.6 copy.91
  141.2 5.9 fusion.15
  155.8 39.5 %collective-permute-done = f32[128,3,1,32,128]{0,3,4,1,2:T(8,128)} collective-permute-done((f32[128,3,1,32,128]{0,3,4,1,2:T(8,128)}, f32[128,3,1,32,128]{0,3,4,1,2:T(8,128)}, u32[]{:S(2)}, u32[]{:S(2)}) %collective-permute-start) | collective-permute-done | bytes 6291488 | tf_op jit(solution)/shard_map/ppermute | solution.py:17
  199.3 6.2 multiply_bitcast_fusion
  207.6 21.6 %copy.87 = f32[128,3,3,1,32,128]{0,5,4,2,1,3:T(8,128)} copy(f32[128,3,3,1,32,128]{0,4,5,2,3,1:T(8,128)S(1)} %pad_maximum_fusion) | data formatting | bytes 37748736 | tf_op jit(solution)/shard_map/stack | solution.py:26
  229.3 18.6 %copy.89 = f32[128,36864]{1,0:T(8,128)} copy(f32[128,36864]{0,1:T(8,128)} %bitcast.87) | data formatting | bytes 37748736 | tf_op jit(solution)/shard_map/while | solution.py:61
  247.9 446.9 %while.10 = (s32[]{:T(128)}, f32[8,64,128]{2,1,0:T(8,128)S(1)}, s32[8,64,2]{1,0,2:T(8,128)S(1)}, f32[128,36864]{1,0:T(8,128)}, f32[128,12288]{1,0:T(8,128)}, /*index=5*/f32[128,3,4096]{2,0,1:T(8,128)}, s32[]{:T(128)}) while((s32[]{:T(128)}, f32[8,64,128]{2,1,0:T(8,128)S(1)}, s32[8,64,2]{1,0,2:T(8,128)S(1)}, f32[128,36864]{1,0:T(8,128)}, ...), condition=%wide.region_1.2_spmd, body=%wide.region_0.1_spmd.sunk | while | flops 6043746304 | bytes 89164368 | solution.py:61
  247.9 13.5 %fusion.35 = f32[64,36864]{1,0:T(8,128)} fusion(f32[128,36864]{1,0:T(8,128)} %get-tuple-element.144, s32[64]{0:T(128)S(1)} %get-tuple-element.125), kind=kOutput, calls=%fused_computation.8.clone.1 | convolution fusion | flops 3623886848 | bytes 28311808 | tf_op jit(solution)/shard_map/while/body/eval_jaxpr/dot_general | solution.py:39
  261.4 12.6 %reshape.112 = f32[64,3,3,4096]{3,2,1,0:T(4,128)} reshape(f32[64,36864]{1,0:T(8,128)} %fusion.35) | data formatting | bytes 18874368 | tf_op jit(solution)/shard_map/while/body/eval_jaxpr/reshape | solution.py:44
  274.0 4.5 fusion.36
  282.3 12.6 %multiply_reduce_fusion.2 = f32[64,4096,3]{1,2,0:T(4,128)S(1)} fusion(f32[64,3,3,4096]{3,2,1,0:T(4,128)} %reshape.112, f32[64,4096,3]{1,2,0:T(4,128)} %bitcast.83), kind=kLoop, calls=%fused_computation.clone.1 | loop fusion | flops 3932160 | bytes 15728640 | tf_op jit(solution)/shard_map/while
  294.8 8.9 %fusion.37 = f32[8,64,128]{2,1,0:T(8,128)S(1)} fusion(f32[8,64,128]{2,1,0:T(8,128)S(1)} %get-tuple-element.135, s32[]{:T(128)} %get-tuple-element.134, f32[128,3,4096]{2,0,1:T(8,128)} %get-tuple-element.146, f32[64,4096,3]{1,2,0:T(4,128)S(1)} %multiply_reduce_fusion.2), kind=kOutput, calls=%fused_computation.5.clone.1 | convolution fusion | flops 1207959552 | bytes 10518532 | tf_op jit(solution)/shard_map/while/body/eval_jaxpr/bcl,kcl->bk/dot_general | solution.py:48
  303.8 13.5 %fusion.35 = f32[64,36864]{1,0:T(8,128)} fusion(f32[128,36864]{1,0:T(8,128)} %get-tuple-element.144, s32[64]{0:T(128)S(1)} %get-tuple-element.125), kind=kOutput, calls=%fused_computation.8.clone.1 | convolution fusion | flops 3623886848 | bytes 28311808 | tf_op jit(solution)/shard_map/while/body/eval_jaxpr/dot_general | solution.py:39
  317.3 12.6 %reshape.112 = f32[64,3,3,4096]{3,2,1,0:T(4,128)} reshape(f32[64,36864]{1,0:T(8,128)} %fusion.35) | data formatting | bytes 18874368 | tf_op jit(solution)/shard_map/while/body/eval_jaxpr/reshape | solution.py:44
  329.8 4.5 fusion.36
  338.1 12.6 %multiply_reduce_fusion.2 = f32[64,4096,3]{1,2,0:T(4,128)S(1)} fusion(f32[64,3,3,4096]{3,2,1,0:T(4,128)} %reshape.112, f32[64,4096,3]{1,2,0:T(4,128)} %bitcast.83), kind=kLoop, calls=%fused_computation.clone.1 | loop fusion | flops 3932160 | bytes 15728640 | tf_op jit(solution)/shard_map/while
  350.7 8.9 %fusion.37 = f32[8,64,128]{2,1,0:T(8,128)S(1)} fusion(f32[8,64,128]{2,1,0:T(8,128)S(1)} %get-tuple-element.135, s32[]{:T(128)} %get-tuple-element.134, f32[128,3,4096]{2,0,1:T(8,128)} %get-tuple-element.146, f32[64,4096,3]{1,2,0:T(4,128)S(1)} %multiply_reduce_fusion.2), kind=kOutput, calls=%fused_computation.5.clone.1 | convolution fusion | flops 1207959552 | bytes 10518532 | tf_op jit(solution)/shard_map/while/body/eval_jaxpr/bcl,kcl->bk/dot_general | solution.py:48
  359.6 13.5 %fusion.35 = f32[64,36864]{1,0:T(8,128)} fusion(f32[128,36864]{1,0:T(8,128)} %get-tuple-element.144, s32[64]{0:T(128)S(1)} %get-tuple-element.125), kind=kOutput, calls=%fused_computation.8.clone.1 | convolution fusion | flops 3623886848 | bytes 28311808 | tf_op jit(solution)/shard_map/while/body/eval_jaxpr/dot_general | solution.py:39
  373.1 12.6 %reshape.112 = f32[64,3,3,4096]{3,2,1,0:T(4,128)} reshape(f32[64,36864]{1,0:T(8,128)} %fusion.35) | data formatting | bytes 18874368 | tf_op jit(solution)/shard_map/while/body/eval_jaxpr/reshape | solution.py:44
  385.7 4.5 fusion.36
  394.0 12.6 %multiply_reduce_fusion.2 = f32[64,4096,3]{1,2,0:T(4,128)S(1)} fusion(f32[64,3,3,4096]{3,2,1,0:T(4,128)} %reshape.112, f32[64,4096,3]{1,2,0:T(4,128)} %bitcast.83), kind=kLoop, calls=%fused_computation.clone.1 | loop fusion | flops 3932160 | bytes 15728640 | tf_op jit(solution)/shard_map/while
  406.6 8.9 %fusion.37 = f32[8,64,128]{2,1,0:T(8,128)S(1)} fusion(f32[8,64,128]{2,1,0:T(8,128)S(1)} %get-tuple-element.135, s32[]{:T(128)} %get-tuple-element.134, f32[128,3,4096]{2,0,1:T(8,128)} %get-tuple-element.146, f32[64,4096,3]{1,2,0:T(4,128)S(1)} %multiply_reduce_fusion.2), kind=kOutput, calls=%fused_computation.5.clone.1 | convolution fusion | flops 1207959552 | bytes 10518532 | tf_op jit(solution)/shard_map/while/body/eval_jaxpr/bcl,kcl->bk/dot_general | solution.py:48
  415.5 13.5 %fusion.35 = f32[64,36864]{1,0:T(8,128)} fusion(f32[128,36864]{1,0:T(8,128)} %get-tuple-element.144, s32[64]{0:T(128)S(1)} %get-tuple-element.125), kind=kOutput, calls=%fused_computation.8.clone.1 | convolution fusion | flops 3623886848 | bytes 28311808 | tf_op jit(solution)/shard_map/while/body/eval_jaxpr/dot_general | solution.py:39
  429.0 12.6 %reshape.112 = f32[64,3,3,4096]{3,2,1,0:T(4,128)} reshape(f32[64,36864]{1,0:T(8,128)} %fusion.35) | data formatting | bytes 18874368 | tf_op jit(solution)/shard_map/while/body/eval_jaxpr/reshape | solution.py:44
  441.6 4.5 fusion.36
  449.9 12.6 %multiply_reduce_fusion.2 = f32[64,4096,3]{1,2,0:T(4,128)S(1)} fusion(f32[64,3,3,4096]{3,2,1,0:T(4,128)} %reshape.112, f32[64,4096,3]{1,2,0:T(4,128)} %bitcast.83), kind=kLoop, calls=%fused_computation.clone.1 | loop fusion | flops 3932160 | bytes 15728640 | tf_op jit(solution)/shard_map/while
  462.4 8.9 %fusion.37 = f32[8,64,128]{2,1,0:T(8,128)S(1)} fusion(f32[8,64,128]{2,1,0:T(8,128)S(1)} %get-tuple-element.135, s32[]{:T(128)} %get-tuple-element.134, f32[128,3,4096]{2,0,1:T(8,128)} %get-tuple-element.146, f32[64,4096,3]{1,2,0:T(4,128)S(1)} %multiply_reduce_fusion.2), kind=kOutput, calls=%fused_computation.5.clone.1 | convolution fusion | flops 1207959552 | bytes 10518532 | tf_op jit(solution)/shard_map/while/body/eval_jaxpr/bcl,kcl->bk/dot_general | solution.py:48
  471.3 13.5 %fusion.35 = f32[64,36864]{1,0:T(8,128)} fusion(f32[128,36864]{1,0:T(8,128)} %get-tuple-element.144, s32[64]{0:T(128)S(1)} %get-tuple-element.125), kind=kOutput, calls=%fused_computation.8.clone.1 | convolution fusion | flops 3623886848 | bytes 28311808 | tf_op jit(solution)/shard_map/while/body/eval_jaxpr/dot_general | solution.py:39
  484.9 12.6 %reshape.112 = f32[64,3,3,4096]{3,2,1,0:T(4,128)} reshape(f32[64,36864]{1,0:T(8,128)} %fusion.35) | data formatting | bytes 18874368 | tf_op jit(solution)/shard_map/while/body/eval_jaxpr/reshape | solution.py:44
  505.7 12.6 %multiply_reduce_fusion.2 = f32[64,4096,3]{1,2,0:T(4,128)S(1)} fusion(f32[64,3,3,4096]{3,2,1,0:T(4,128)} %reshape.112, f32[64,4096,3]{1,2,0:T(4,128)} %bitcast.83), kind=kLoop, calls=%fused_computation.clone.1 | loop fusion | flops 3932160 | bytes 15728640 | tf_op jit(solution)/shard_map/while
  518.3 8.9 %fusion.37 = f32[8,64,128]{2,1,0:T(8,128)S(1)} fusion(f32[8,64,128]{2,1,0:T(8,128)S(1)} %get-tuple-element.135, s32[]{:T(128)} %get-tuple-element.134, f32[128,3,4096]{2,0,1:T(8,128)} %get-tuple-element.146, f32[64,4096,3]{1,2,0:T(4,128)S(1)} %multiply_reduce_fusion.2), kind=kOutput, calls=%fused_computation.5.clone.1 | convolution fusion | flops 1207959552 | bytes 10518532 | tf_op jit(solution)/shard_map/while/body/eval_jaxpr/bcl,kcl->bk/dot_general | solution.py:48
  527.2 13.5 %fusion.35 = f32[64,36864]{1,0:T(8,128)} fusion(f32[128,36864]{1,0:T(8,128)} %get-tuple-element.144, s32[64]{0:T(128)S(1)} %get-tuple-element.125), kind=kOutput, calls=%fused_computation.8.clone.1 | convolution fusion | flops 3623886848 | bytes 28311808 | tf_op jit(solution)/shard_map/while/body/eval_jaxpr/dot_general | solution.py:39
  540.7 12.6 %reshape.112 = f32[64,3,3,4096]{3,2,1,0:T(4,128)} reshape(f32[64,36864]{1,0:T(8,128)} %fusion.35) | data formatting | bytes 18874368 | tf_op jit(solution)/shard_map/while/body/eval_jaxpr/reshape | solution.py:44
  561.6 12.6 %multiply_reduce_fusion.2 = f32[64,4096,3]{1,2,0:T(4,128)S(1)} fusion(f32[64,3,3,4096]{3,2,1,0:T(4,128)} %reshape.112, f32[64,4096,3]{1,2,0:T(4,128)} %bitcast.83), kind=kLoop, calls=%fused_computation.clone.1 | loop fusion | flops 3932160 | bytes 15728640 | tf_op jit(solution)/shard_map/while
  574.2 8.9 %fusion.37 = f32[8,64,128]{2,1,0:T(8,128)S(1)} fusion(f32[8,64,128]{2,1,0:T(8,128)S(1)} %get-tuple-element.135, s32[]{:T(128)} %get-tuple-element.134, f32[128,3,4096]{2,0,1:T(8,128)} %get-tuple-element.146, f32[64,4096,3]{1,2,0:T(4,128)S(1)} %multiply_reduce_fusion.2), kind=kOutput, calls=%fused_computation.5.clone.1 | convolution fusion | flops 1207959552 | bytes 10518532 | tf_op jit(solution)/shard_map/while/body/eval_jaxpr/bcl,kcl->bk/dot_general | solution.py:48
  583.1 13.5 %fusion.35 = f32[64,36864]{1,0:T(8,128)} fusion(f32[128,36864]{1,0:T(8,128)} %get-tuple-element.144, s32[64]{0:T(128)S(1)} %get-tuple-element.125), kind=kOutput, calls=%fused_computation.8.clone.1 | convolution fusion | flops 3623886848 | bytes 28311808 | tf_op jit(solution)/shard_map/while/body/eval_jaxpr/dot_general | solution.py:39
  596.6 12.6 %reshape.112 = f32[64,3,3,4096]{3,2,1,0:T(4,128)} reshape(f32[64,36864]{1,0:T(8,128)} %fusion.35) | data formatting | bytes 18874368 | tf_op jit(solution)/shard_map/while/body/eval_jaxpr/reshape | solution.py:44
  617.4 12.6 %multiply_reduce_fusion.2 = f32[64,4096,3]{1,2,0:T(4,128)S(1)} fusion(f32[64,3,3,4096]{3,2,1,0:T(4,128)} %reshape.112, f32[64,4096,3]{1,2,0:T(4,128)} %bitcast.83), kind=kLoop, calls=%fused_computation.clone.1 | loop fusion | flops 3932160 | bytes 15728640 | tf_op jit(solution)/shard_map/while
  630.0 8.9 %fusion.37 = f32[8,64,128]{2,1,0:T(8,128)S(1)} fusion(f32[8,64,128]{2,1,0:T(8,128)S(1)} %get-tuple-element.135, s32[]{:T(128)} %get-tuple-element.134, f32[128,3,4096]{2,0,1:T(8,128)} %get-tuple-element.146, f32[64,4096,3]{1,2,0:T(4,128)S(1)} %multiply_reduce_fusion.2), kind=kOutput, calls=%fused_computation.5.clone.1 | convolution fusion | flops 1207959552 | bytes 10518532 | tf_op jit(solution)/shard_map/while/body/eval_jaxpr/bcl,kcl->bk/dot_general | solution.py:48
  638.9 13.5 %fusion.35 = f32[64,36864]{1,0:T(8,128)} fusion(f32[128,36864]{1,0:T(8,128)} %get-tuple-element.144, s32[64]{0:T(128)S(1)} %get-tuple-element.125), kind=kOutput, calls=%fused_computation.8.clone.1 | convolution fusion | flops 3623886848 | bytes 28311808 | tf_op jit(solution)/shard_map/while/body/eval_jaxpr/dot_general | solution.py:39
  652.5 12.6 %reshape.112 = f32[64,3,3,4096]{3,2,1,0:T(4,128)} reshape(f32[64,36864]{1,0:T(8,128)} %fusion.35) | data formatting | bytes 18874368 | tf_op jit(solution)/shard_map/while/body/eval_jaxpr/reshape | solution.py:44
  673.3 12.6 %multiply_reduce_fusion.2 = f32[64,4096,3]{1,2,0:T(4,128)S(1)} fusion(f32[64,3,3,4096]{3,2,1,0:T(4,128)} %reshape.112, f32[64,4096,3]{1,2,0:T(4,128)} %bitcast.83), kind=kLoop, calls=%fused_computation.clone.1 | loop fusion | flops 3932160 | bytes 15728640 | tf_op jit(solution)/shard_map/while
  685.9 8.9 %fusion.37 = f32[8,64,128]{2,1,0:T(8,128)S(1)} fusion(f32[8,64,128]{2,1,0:T(8,128)S(1)} %get-tuple-element.135, s32[]{:T(128)} %get-tuple-element.134, f32[128,3,4096]{2,0,1:T(8,128)} %get-tuple-element.146, f32[64,4096,3]{1,2,0:T(4,128)S(1)} %multiply_reduce_fusion.2), kind=kOutput, calls=%fused_computation.5.clone.1 | convolution fusion | flops 1207959552 | bytes 10518532 | tf_op jit(solution)/shard_map/while/body/eval_jaxpr/bcl,kcl->bk/dot_general | solution.py:48
  695.5 55.9 %reduce-scatter.2.cloned.1.call-done = f32[32,128]{1,0:T(8,128)} async-done(((f32[512,128]{1,0:T(8,128)}), f32[32,128]{1,0:T(8,128)}) %reduce-scatter.2.cloned.1.call-update) | async-done | bytes 16400 | tf_op jit(solution)/shard_map/reduce_scatter | solution.py:89
  (55 shorter events, 73.1 us)
Async XLA Ops:
  6.5 33.0 %copy-start = (f32[256,128]{1,0:T(8,128)S(1)}, f32[256,128]{1,0:T(8,128)}, u32[]{:S(2)}) copy-start(f32[256,128]{1,0:T(8,128)} %param.6) | copy-start | bytes 393220
  6.5 744.9 %reduce-scatter.2.cloned.1.call-start = ((), (), s32[]{:S(2)}) async-start(), calls=%async_computation.3 | async-start | bytes 278528 | tf_op jit(solution)/shard_map/reduce_scatter | solution.py:89
  118.3 6.7 copy-start.2
  125.0 70.3 %collective-permute-start = (f32[128,3,1,32,128]{0,3,4,1,2:T(8,128)}, f32[128,3,1,32,128]{0,3,4,1,2:T(8,128)}, u32[]{:S(2)}, u32[]{:S(2)}) collective-permute-start(f32[128,3,1,32,128]{0,3,4,1,2:T(8,128)} %bitcast.14), channel_id=1, source_target_pairs={{1,0},{2,1},{3,2},{4,3},{5,4},{6,5},{7,6},{8,7},{9,8},{10,9},{11,1... | collective-permute-start | bytes 18874376 | tf_op jit(solution)/shard_map/ppermute | solution.py:17
  126.5 72.8 %collective-permute-start.1 = (f32[128,3,1,32,128]{0,3,4,1,2:T(8,128)}, f32[128,3,1,32,128]{0,3,4,1,2:T(8,128)}, u32[]{:S(2)}, u32[]{:S(2)}) collective-permute-start(f32[128,3,1,32,128]{0,3,4,1,2:T(8,128)} %bitcast.14), channel_id=1, source_target_pairs={{0,1},{1,2},{2,3},{3,4},{4,5},{5,6},{6,7},{7,8},{8,9},{9,10},{10,1... | collective-permute-start | bytes 18874376 | tf_op jit(solution)/shard_map/ppermute | solution.py:14
  694.8 56.7 %copy-start.1 = (f32[256,128]{1,0:T(8,128)S(1)}, f32[256,128]{1,0:T(8,128)}, u32[]{:S(2)}) copy-start(f32[256,128]{1,0:T(8,128)} %param.6) | copy-start | bytes 393220
Sparse Core Ops, SparseCore 0:
  695.7 55.7 reduce-scatter.1
